TPU v7x, 32 devices: a whole 2x2x4 slice. The times are simulated.
32 devices in a mesh: groups: 2 (over y), row: 4 (over z), col: 4 (over x, core).
Axes of the slice: x: 2, y: 2, z: 4, core: 2. Of those that a mesh axis runs over, the one named last changes fastest.
Arguments:
- queries: bfloat16 [4096, 1024], P(('groups', 'row'), 'col'), parts along dimension 0, may hold values from -64 to 64
- keys: bfloat16 [4096, 1024], P(('groups', 'col'), 'row'), parts along dimension 0, may hold values from -6 to 6
- values: bfloat16 [4096, 1024], P(('groups', 'col'), 'row'), parts along dimension 0, may hold values from -6 to 6
- cotangent: bfloat16 [4096, 1024], P(('groups', 'row'), 'col'), parts along dimension 0, may hold values from -6 to 6
- block_lists: int32 [32, 16], P(('groups', 'row')), parts along dimension 0, may hold values from 0 to 15, as said below
- block_counts: int32 [32], P(('groups', 'row')), parts along dimension 0, may hold values from 1 to 16, as said below
Outputs:
- attended: bfloat16 [4096, 1024], P(('groups', 'row'), 'col'), parts along dimension 0
- grad_queries: bfloat16 [4096, 1024], P(('groups', 'row'), 'col'), parts along dimension 0
- grad_keys: bfloat16 [4096, 1024], P(('groups', 'col'), 'row'), parts along dimension 0
- grad_values: bfloat16 [4096, 1024], P(('groups', 'col'), 'row'), parts along dimension 0
There are 2 independent parts, one for each index of `groups`. A program takes and returns all parts, laid end to end along the dimension named above; each array names one. Nothing has to cross between parts.
Inputs may be any that keep to these rules, and one draw needn't show every extreme that they name: `block_lists`: each row lists 16 distinct blocks; its first entry is the query block itself. `block_counts`: some query block has all 16 entries live in every draw.
All inputs are finite; a program needn't handle non-finite values.
Results may differ from a plain program's by a relative error of at most 0.011.
Values may be sent and summed in bfloat16 or wider, within the bound.
No kernel may reach another device: no remote copies, remote signals or barrier semaphores. Data moves between devices by JAX's collectives and lax.ppermute only.
A program may use at most 64 MiB of HBM per device.

v0:
```python
import math
import jax
import jax.numpy as jnp
from jax import lax
from jax.sharding import PartitionSpec as P

D = 1024
HEADS = 16
HEAD = 64
BLK = 128
MAXNB = 16
NEG_FILL = -1e30


def tile_scores(query_tile, key_tile, score_scale):
    query_heads = query_tile.reshape(query_tile.shape[0], HEADS, -1)
    key_heads = key_tile.reshape(key_tile.shape[0], HEADS, -1)
    return (
        jnp.einsum("qhd,khd->hqk", query_heads, key_heads, preferred_element_type=jnp.float32)
        * score_scale
    )


def on_device(queries, keys, values, cotangent, block_lists, block_counts):
    score_scale = 1.0 / math.sqrt(HEAD)
    q_full = lax.all_gather(queries, "col", axis=1, tiled=True)
    k_full, v_full = (
        lax.all_gather(keys, "row", axis=1, tiled=True),
        lax.all_gather(values, "row", axis=1, tiled=True),
    )
    q_rows = q_full.shape[0]
    k_rows = k_full.shape[0]
    q_blocks = q_rows // BLK
    k_blocks = k_rows // BLK
    group_size = min(4, q_blocks)
    span_rows = group_size * BLK
    supers = q_blocks // group_size
    tile_count = supers * k_blocks
    first_key = lax.axis_index("col") * k_blocks
    wanted = first_key + jnp.arange(k_blocks, dtype=jnp.int32)
    live_slots = jnp.arange(MAXNB, dtype=jnp.int32)[None, :] < block_counts[:, None]
    block_hit = jnp.any(
        (block_lists[:, :, None] == wanted[None, None, :]) & live_slots[:, :, None], axis=1
    )
    block_hit = block_hit.reshape(supers, group_size, k_blocks).transpose(0, 2, 1)
    row_mask = jnp.repeat(block_hit, BLK, axis=2)
    tile_any = jnp.any(block_hit, axis=2)

    def tile_parts(step):
        super_at = step // k_blocks
        key_at = step % k_blocks
        query_tile = lax.dynamic_slice_in_dim(q_full, super_at * span_rows, span_rows, 0)
        key_tile = lax.dynamic_slice_in_dim(k_full, key_at * BLK, BLK, 0)
        value_tile = lax.dynamic_slice_in_dim(v_full, key_at * BLK, BLK, 0)
        keep_mask = row_mask[super_at, key_at][None, :, None]
        return (super_at, key_at, query_tile, key_tile, value_tile, keep_mask)

    def unchanged(carry):
        return carry

    def stats_step(step, carry):
        super_at, key_at, query_tile, key_tile, value_tile, keep_mask = tile_parts(step)

        def stats_work(state):
            row_top, row_total = state
            scores = jnp.where(keep_mask, tile_scores(query_tile, key_tile, score_scale), NEG_FILL)
            old_top = lax.dynamic_slice_in_dim(row_top, super_at * span_rows, span_rows, 1)
            old_total = lax.dynamic_slice_in_dim(row_total, super_at * span_rows, span_rows, 1)
            new_top = jnp.maximum(old_top, jnp.max(scores, axis=2))
            exp_terms = jnp.where(keep_mask, jnp.exp(scores - new_top[:, :, None]), 0.0)
            fresh = old_total * jnp.exp(old_top - new_top) + jnp.sum(exp_terms, axis=2)
            return (
                lax.dynamic_update_slice_in_dim(row_top, new_top, super_at * span_rows, 1),
                lax.dynamic_update_slice_in_dim(row_total, fresh, super_at * span_rows, 1),
            )

        return lax.cond(tile_any[super_at, key_at], stats_work, unchanged, carry)

    start_top = jnp.full((HEADS, q_rows), NEG_FILL, jnp.float32)
    start_total = jnp.zeros((HEADS, q_rows), jnp.float32)
    local_top, local_total = lax.fori_loop(0, tile_count, stats_step, (start_top, start_total))
    row_top = lax.pmax(local_top.astype(jnp.bfloat16), "col").astype(local_top.dtype)
    row_total = lax.psum(local_total * jnp.exp(local_top - row_top), "col")

    def tile_weights(scores, super_at, keep_mask):
        top_rows = lax.dynamic_slice_in_dim(row_top, super_at * span_rows, span_rows, 1)
        total_rows = lax.dynamic_slice_in_dim(row_total, super_at * span_rows, span_rows, 1)
        ratio = jnp.exp(scores - top_rows[:, :, None]) / total_rows[:, :, None]
        return jnp.where(keep_mask, ratio, 0.0).astype(jnp.bfloat16)

    def output_step(step, carry):
        super_at, key_at, query_tile, key_tile, value_tile, keep_mask = tile_parts(step)

        def output_work(out_rows):
            scores = jnp.where(keep_mask, tile_scores(query_tile, key_tile, score_scale), NEG_FILL)
            weights = tile_weights(scores, super_at, keep_mask)
            value_heads = value_tile.reshape(BLK, HEADS, -1)
            part = jnp.einsum(
                "hqk,khd->qhd", weights, value_heads, preferred_element_type=jnp.float32
            ).reshape(span_rows, -1)
            current = lax.dynamic_slice_in_dim(out_rows, super_at * span_rows, span_rows, 0)
            return lax.dynamic_update_slice_in_dim(
                out_rows, current + part, super_at * span_rows, 0
            )

        return lax.cond(tile_any[super_at, key_at], output_work, unchanged, carry)

    partial_out = lax.fori_loop(0, tile_count, output_step, jnp.zeros((q_rows, D), jnp.float32))
    out_share = lax.psum_scatter(partial_out, "col", scatter_dimension=1, tiled=True).astype(
        jnp.bfloat16
    )
    grad_full, out_full = (
        lax.all_gather(cotangent, "col", axis=1, tiled=True),
        lax.all_gather(out_share, "col", axis=1, tiled=True),
    )
    delta = jnp.einsum(
        "qhd,qhd->hq",
        grad_full.reshape(q_rows, HEADS, -1),
        out_full.reshape(q_rows, HEADS, -1),
        preferred_element_type=jnp.float32,
    )

    def grad_step(step, carry):
        super_at, key_at, query_tile, key_tile, value_tile, keep_mask = tile_parts(step)

        def grad_work(state):
            query_accum, key_accum, value_accum = state
            scores = jnp.where(keep_mask, tile_scores(query_tile, key_tile, score_scale), NEG_FILL)
            weights = tile_weights(scores, super_at, keep_mask)
            grad_tile = lax.dynamic_slice_in_dim(
                grad_full, super_at * span_rows, span_rows, 0
            ).reshape(span_rows, HEADS, -1)
            value_heads = value_tile.reshape(BLK, HEADS, -1)
            key_heads = key_tile.reshape(BLK, HEADS, -1)
            query_heads = query_tile.reshape(span_rows, HEADS, -1)
            dweights = jnp.einsum(
                "qhd,khd->hqk", grad_tile, value_heads, preferred_element_type=jnp.float32
            )
            delta_rows = lax.dynamic_slice_in_dim(delta, super_at * span_rows, span_rows, 1)
            dscores = (weights.astype(jnp.float32) * (dweights - delta_rows[:, :, None])).astype(
                jnp.bfloat16
            )
            query_part = score_scale * jnp.einsum(
                "hqk,khd->qhd", dscores, key_heads, preferred_element_type=jnp.float32
            )
            key_part = score_scale * jnp.einsum(
                "hqk,qhd->khd", dscores, query_heads, preferred_element_type=jnp.float32
            )
            value_part = jnp.einsum(
                "hqk,qhd->khd", weights, grad_tile, preferred_element_type=jnp.float32
            )
            query_now = lax.dynamic_slice_in_dim(query_accum, super_at * span_rows, span_rows, 0)
            key_now = lax.dynamic_slice_in_dim(key_accum, key_at * BLK, BLK, 0)
            value_now = lax.dynamic_slice_in_dim(value_accum, key_at * BLK, BLK, 0)
            query_accum = lax.dynamic_update_slice_in_dim(
                query_accum, query_now + query_part.reshape(span_rows, -1), super_at * span_rows, 0
            )
            key_accum = lax.dynamic_update_slice_in_dim(
                key_accum, key_now + key_part.reshape(BLK, -1), key_at * BLK, 0
            )
            value_accum = lax.dynamic_update_slice_in_dim(
                value_accum, value_now + value_part.reshape(BLK, -1), key_at * BLK, 0
            )
            return (query_accum, key_accum, value_accum)

        return lax.cond(tile_any[super_at, key_at], grad_work, unchanged, carry)

    start_grads = (
        jnp.zeros((q_rows, D), jnp.float32),
        jnp.zeros((k_rows, D), jnp.float32),
        jnp.zeros((k_rows, D), jnp.float32),
    )
    query_parts, key_parts, value_parts = lax.fori_loop(0, tile_count, grad_step, start_grads)
    grad_queries = lax.psum_scatter(query_parts, "col", scatter_dimension=1, tiled=True).astype(
        jnp.bfloat16
    )
    grad_keys, grad_values = (
        lax.psum_scatter(key_parts, "row", scatter_dimension=1, tiled=True),
        lax.psum_scatter(value_parts, "row", scatter_dimension=1, tiled=True),
    )
    return (
        out_share,
        grad_queries,
        grad_keys.astype(jnp.bfloat16),
        grad_values.astype(jnp.bfloat16),
    )


def solution(mesh):
    return jax.shard_map(
        on_device,
        mesh=mesh,
        in_specs=(
            P(("groups", "row"), "col"),
            P(("groups", "col"), "row"),
            P(("groups", "col"), "row"),
            P(("groups", "row"), "col"),
            P(("groups", "row"), None),
            P(("groups", "row")),
        ),
        out_specs=(
            P(("groups", "row"), "col"),
            P(("groups", "row"), "col"),
            P(("groups", "col"), "row"),
            P(("groups", "col"), "row"),
        ),
        check_vma=False,
    )
```

profile of v0, /device:TPU:0, one launch (start us, length us, event | category | flops | bytes accessed | tf_op | source)
XLA Modules:
  0.0 402.9 jit_solution(14908098541145584658)
XLA Ops:
  13.3 16.3 %all-gather.8.cloned.1.call-done = bf16[512,1024]{0,1:T(8,128)(2,1)} async-done(((bf16[512,256]{0,1:T(8,128)(2,1)}), bf16[512,1024]{0,1:T(8,128)(2,1)}) %all-gather.8.cloned.1.call-update) | async-done | bytes 1048592 | tf_op jit(solution)/shard_map/all_gather | solution.py:26
  29.6 30.1 %all-gather.6.cloned.1.call-done = bf16[512,1024]{0,1:T(8,128)(2,1)} async-done(((bf16[512,256]{0,1:T(8,128)(2,1)}), bf16[512,1024]{0,1:T(8,128)(2,1)}) %all-gather.6.cloned.1.call-update) | async-done | bytes 1048592 | tf_op jit(solution)/shard_map/all_gather | solution.py:28
  59.7 21.9 %while.57 = (s32[]{:T(128)}, f32[16,512]{1,0:T(8,128)S(1)}, f32[16,512]{1,0:T(8,128)S(1)}, pred[1,4]{1,0:T(4,128)(4,1)S(1)}, bf16[512,1024]{0,1:T(8,128)(2,1)}, ...) while((s32[]{:T(128)}, f32[16,512]{1,0:T(8,128)S(1)}, ...), condition=%wide.region_7.8_spmd.clone, body=%wide.region_2.7_spmd.clone.sunk | while | flops 142622736 | bytes 10658168 | solution.py:81
  65.8 4.9 %conditional.9 = ((f32[16,512]{1,0:T(8,128)S(1)}, f32[16,512]{1,0:T(8,128)S(1)})) conditional(s32[]{:T(128)} %bitcast.68, (f32[16,512]{1,0:T(8,128)S(1)}, f32[16,512]{1,0:T(8,128)S(1)}) %tuple.194, (pred[4,4]{1,0:T(4,128)(4,1)S(1)}, s32[]{:T(128)}, s32[]{:T(128)}, bf16[512,1024]{0,1:T(8,128)(2,1)}, bf16[512,1024]{0,1:T(8,128)(2,1)}, ...), branch_computations={%region_3.3_spmd, %region_4.6_spmd} | conditional | flops 142622720 | bytes 10657886 | solution.py:77
  71.3 4.8 %conditional.9 = ((f32[16,512]{1,0:T(8,128)S(1)}, f32[16,512]{1,0:T(8,128)S(1)})) conditional(s32[]{:T(128)} %bitcast.68, (f32[16,512]{1,0:T(8,128)S(1)}, f32[16,512]{1,0:T(8,128)S(1)}) %tuple.194, (pred[4,4]{1,0:T(4,128)(4,1)S(1)}, s32[]{:T(128)}, s32[]{:T(128)}, bf16[512,1024]{0,1:T(8,128)(2,1)}, bf16[512,1024]{0,1:T(8,128)(2,1)}, ...), branch_computations={%region_3.3_spmd, %region_4.6_spmd} | conditional | flops 142622720 | bytes 10657886 | solution.py:77
  76.8 4.8 %conditional.9 = ((f32[16,512]{1,0:T(8,128)S(1)}, f32[16,512]{1,0:T(8,128)S(1)})) conditional(s32[]{:T(128)} %bitcast.68, (f32[16,512]{1,0:T(8,128)S(1)}, f32[16,512]{1,0:T(8,128)S(1)}) %tuple.194, (pred[4,4]{1,0:T(4,128)(4,1)S(1)}, s32[]{:T(128)}, s32[]{:T(128)}, bf16[512,1024]{0,1:T(8,128)(2,1)}, bf16[512,1024]{0,1:T(8,128)(2,1)}, ...), branch_computations={%region_3.3_spmd, %region_4.6_spmd} | conditional | flops 142622720 | bytes 10657886 | solution.py:77
  81.6 11.3 %pmax.7 = bf16[16,512]{1,0:T(8,128)(2,1)S(1)} all-reduce(bf16[16,512]{1,0:T(8,128)(2,1)S(1)} %convert_element_type.89), channel_id=1, replica_groups=mesh['groups'=2,'row'=4,'col'=4] {'col'}, use_global_device_ids=true, to_apply=%region_8.9 | all-reduce | flops 8192 | bytes 32768 | tf_op jit(solution)/shard_map/pmax | solution.py:82
  92.9 10.3 %psum.7 = f32[16,512]{1,0:T(8,128)S(1)} all-reduce(f32[16,512]{1,0:T(8,128)S(1)} %exponential_multiply_fusion), channel_id=1, replica_groups=mesh['groups'=2,'row'=4,'col'=4] {'col'}, use_global_device_ids=true, to_apply=%region_9.10 | all-reduce | flops 8192 | bytes 65536 | tf_op jit(solution)/shard_map/psum | solution.py:83
  103.5 36.9 %while.58 = (s32[]{:T(128)}, f32[512,1024]{0,1:T(8,128)S(1)}, pred[1,4]{1,0:T(4,128)(4,1)S(1)}, bf16[512,1024]{0,1:T(8,128)(2,1)}, bf16[512,1024]{0,1:T(8,128)(2...) while((s32[]{:T(128)}, f32[512,1024]{0,1:T(8,128)S(1)}, ...), condition=%wide.region_13.14_spmd.clone, body=%wide.region_10.13_spmd.clone.sunk | while | flops 275251200 | bytes 11083640 | solution.py:108
  104.2 8.6 %conditional.10 = (f32[512,1024]{0,1:T(8,128)S(1)}) conditional(s32[]{:T(128)} %bitcast.69, f32[512,1024]{0,1:T(8,128)S(1)} %get-tuple-element.1617, (pred[4,4]{1,0:T(4,128)(4,1)S(1)}, s32[]{:T(128)}, s32[]{:T(128)}, bf16[512,1024]{0,1:T(8,128)(2,1)}, bf16[512,1024]{0,1:T(8,128)(2,1)S(1)}, /*index=5*/f32[16,512]{1,0:T(8,128)S(1)}, ...), branch_computations={%region_11.11_spmd, %region_12.12_spmd} | conditional | flops 275251200 | bytes 11083342 | solution.py:106
  113.4 8.6 %conditional.10 = (f32[512,1024]{0,1:T(8,128)S(1)}) conditional(s32[]{:T(128)} %bitcast.69, f32[512,1024]{0,1:T(8,128)S(1)} %get-tuple-element.1617, (pred[4,4]{1,0:T(4,128)(4,1)S(1)}, s32[]{:T(128)}, s32[]{:T(128)}, bf16[512,1024]{0,1:T(8,128)(2,1)}, bf16[512,1024]{0,1:T(8,128)(2,1)S(1)}, /*index=5*/f32[16,512]{1,0:T(8,128)S(1)}, ...), branch_computations={%region_11.11_spmd, %region_12.12_spmd} | conditional | flops 275251200 | bytes 11083342 | solution.py:106
  122.6 8.6 %conditional.10 = (f32[512,1024]{0,1:T(8,128)S(1)}) conditional(s32[]{:T(128)} %bitcast.69, f32[512,1024]{0,1:T(8,128)S(1)} %get-tuple-element.1617, (pred[4,4]{1,0:T(4,128)(4,1)S(1)}, s32[]{:T(128)}, s32[]{:T(128)}, bf16[512,1024]{0,1:T(8,128)(2,1)}, bf16[512,1024]{0,1:T(8,128)(2,1)S(1)}, /*index=5*/f32[16,512]{1,0:T(8,128)S(1)}, ...), branch_computations={%region_11.11_spmd, %region_12.12_spmd} | conditional | flops 275251200 | bytes 11083342 | solution.py:106
  131.9 8.6 %conditional.10 = (f32[512,1024]{0,1:T(8,128)S(1)}) conditional(s32[]{:T(128)} %bitcast.69, f32[512,1024]{0,1:T(8,128)S(1)} %get-tuple-element.1617, (pred[4,4]{1,0:T(4,128)(4,1)S(1)}, s32[]{:T(128)}, s32[]{:T(128)}, bf16[512,1024]{0,1:T(8,128)(2,1)}, bf16[512,1024]{0,1:T(8,128)(2,1)S(1)}, /*index=5*/f32[16,512]{1,0:T(8,128)S(1)}, ...), branch_computations={%region_11.11_spmd, %region_12.12_spmd} | conditional | flops 275251200 | bytes 11083342 | solution.py:106
  142.8 29.6 %reduce-scatter.5.cloned.1.call-done = f32[512,256]{0,1:T(8,128)} async-done(((f32[512,1024]{0,1:T(8,128)}), f32[512,256]{0,1:T(8,128)}) %reduce-scatter.5.cloned.1.call-update) | async-done | bytes 524304 | tf_op jit(solution)/shard_map/reduce_scatter | solution.py:109
  174.2 17.0 %all-gather.12.cloned.1.call-done = bf16[512,1024]{0,1:T(8,128)(2,1)} async-done(((bf16[512,256]{0,1:T(8,128)(2,1)}), bf16[512,1024]{0,1:T(8,128)(2,1)}) %all-gather.12.cloned.1.call-update) | async-done | bytes 1048592 | tf_op jit(solution)/shard_map/all_gather | solution.py:113
  191.2 18.8 %all-gather.14.cloned.1.call-done = bf16[512,1024]{0,1:T(8,128)(2,1)} async-done(((bf16[512,256]{0,1:T(8,128)(2,1)}), bf16[512,1024]{0,1:T(8,128)(2,1)}) %all-gather.14.cloned.1.call-update) | async-done | bytes 1048592 | tf_op jit(solution)/shard_map/all_gather | solution.py:114
  216.6 51.4 %while.59 = (s32[]{:T(128)}, f32[512,1024]{0,1:T(8,128)}, f32[512,1024]{0,1:T(8,128)}, f32[512,1024]{0,1:T(8,128)}, pred[1,4]{1,0:T(4,128)(4,1)S(1)}, /*index=5*...) while((s32[]{:T(128)}, f32[512,1024]{0,1:T(8,128)}, ...), condition=%wide.region_18.19_spmd.clone, body=%wide.region_15.18_spmd.clone.sunk | while | flops 683016192 | bytes 48078884 | solution.py:173
  217.2 12.3 %conditional.11 = ((f32[512,1024]{0,1:T(8,128)}, f32[512,1024]{0,1:T(8,128)}, f32[512,1024]{0,1:T(8,128)})) conditional(s32[]{:T(128)} %bitcast.70, (f32[512,1024]{0,1:T(8,128)}, f32[512,1024]{0,1:T(8,128)}, f32[512,1024]{0,1:T(8,128)}) %tuple.199, (pred[4,4]{1,0:T(4,128)(4,1)S(1)}, s32[]{:T(128)}, s32[]{:T(128)}, bf16[512,1024]{0,1:T(8,128)(2,1)}, ...), branch_computations={%region_16.16_spmd, %region_17.17_spmd} | conditional | flops 683016192 | bytes 48078500 | solution.py:166
  230.1 12.3 %conditional.11 = ((f32[512,1024]{0,1:T(8,128)}, f32[512,1024]{0,1:T(8,128)}, f32[512,1024]{0,1:T(8,128)})) conditional(s32[]{:T(128)} %bitcast.70, (f32[512,1024]{0,1:T(8,128)}, f32[512,1024]{0,1:T(8,128)}, f32[512,1024]{0,1:T(8,128)}) %tuple.199, (pred[4,4]{1,0:T(4,128)(4,1)S(1)}, s32[]{:T(128)}, s32[]{:T(128)}, bf16[512,1024]{0,1:T(8,128)(2,1)}, ...), branch_computations={%region_16.16_spmd, %region_17.17_spmd} | conditional | flops 683016192 | bytes 48078500 | solution.py:166
  242.9 12.3 %conditional.11 = ((f32[512,1024]{0,1:T(8,128)}, f32[512,1024]{0,1:T(8,128)}, f32[512,1024]{0,1:T(8,128)})) conditional(s32[]{:T(128)} %bitcast.70, (f32[512,1024]{0,1:T(8,128)}, f32[512,1024]{0,1:T(8,128)}, f32[512,1024]{0,1:T(8,128)}) %tuple.199, (pred[4,4]{1,0:T(4,128)(4,1)S(1)}, s32[]{:T(128)}, s32[]{:T(128)}, bf16[512,1024]{0,1:T(8,128)(2,1)}, ...), branch_computations={%region_16.16_spmd, %region_17.17_spmd} | conditional | flops 683016192 | bytes 48078500 | solution.py:166
  255.8 12.3 %conditional.11 = ((f32[512,1024]{0,1:T(8,128)}, f32[512,1024]{0,1:T(8,128)}, f32[512,1024]{0,1:T(8,128)})) conditional(s32[]{:T(128)} %bitcast.70, (f32[512,1024]{0,1:T(8,128)}, f32[512,1024]{0,1:T(8,128)}, f32[512,1024]{0,1:T(8,128)}) %tuple.199, (pred[4,4]{1,0:T(4,128)(4,1)S(1)}, s32[]{:T(128)}, s32[]{:T(128)}, bf16[512,1024]{0,1:T(8,128)(2,1)}, ...), branch_computations={%region_16.16_spmd, %region_17.17_spmd} | conditional | flops 683016192 | bytes 48078500 | solution.py:166
  279.6 35.4 %reduce-scatter.11.cloned.1.call-done = f32[512,256]{1,0:T(8,128)} async-done(((f32[512,1024]{1,0:T(8,128)}), f32[512,256]{1,0:T(8,128)}) %reduce-scatter.11.cloned.1.call-update) | async-done | bytes 524304 | tf_op jit(solution)/shard_map/reduce_scatter | solution.py:179
  316.8 31.5 %reduce-scatter.7.cloned.1.call-done = f32[512,256]{1,0:T(8,128)} async-done(((f32[512,1024]{1,0:T(8,128)}), f32[512,256]{1,0:T(8,128)}) %reduce-scatter.7.cloned.1.call-update) | async-done | bytes 524304 | tf_op jit(solution)/shard_map/reduce_scatter | solution.py:174
  350.1 44.5 %reduce-scatter.9.cloned.1.call-done = f32[512,256]{1,0:T(8,128)} async-done(((f32[512,1024]{1,0:T(8,128)}), f32[512,256]{1,0:T(8,128)}) %reduce-scatter.9.cloned.1.call-update) | async-done | bytes 524304 | tf_op jit(solution)/shard_map/reduce_scatter | solution.py:178
  (200 shorter events, 140.7 us)
Async XLA Ops:
  7.2 5.7 %copy-start.10 = (s32[4]{0:T(128)S(1)}, s32[4]{0:T(128)}, u32[]{:S(2)}) copy-start(s32[4]{0:T(128)} %param.23) | copy-start | bytes 52
  7.2 5.8 %copy-start.9 = (s32[4,16]{1,0:T(4,128)S(1)}, s32[4,16]{1,0:T(4,128)}, u32[]{:S(2)}) copy-start(s32[4,16]{1,0:T(4,128)} %param.22) | copy-start | bytes 772
  7.2 22.4 %all-gather.8.cloned.1.call-start = ((), (), s32[]{:S(2)}) async-start(), calls=%async_computation.5 | async-start | bytes 1310720 | tf_op jit(solution)/shard_map/all_gather | solution.py:26
  9.1 50.7 %all-gather.6.cloned.1.call-start = ((), (), s32[]{:S(2)}) async-start(), calls=%async_computation.4 | async-start | bytes 1310720 | tf_op jit(solution)/shard_map/all_gather | solution.py:28
  10.9 92.3 %all-gather.10.cloned.1.call-start = ((), (), s32[]{:S(2)}) async-start(), calls=%async_computation.6 | async-start | bytes 1310720 | tf_op jit(solution)/shard_map/all_gather | solution.py:29
  12.8 159.5 %reduce-scatter.5.cloned.1.call-start = ((), (), s32[]{:S(2)}) async-start(), calls=%async_computation.7 | async-start | bytes 2621440 | tf_op jit(solution)/shard_map/reduce_scatter | solution.py:109
  81.6 21.9 %copy-start.1 = (bf16[512,1024]{0,1:T(8,128)(2,1)S(1)}, bf16[512,1024]{0,1:T(8,128)(2,1)}, u32[]{:S(2)}) copy-start(bf16[512,1024]{0,1:T(8,128)(2,1)} %get-tuple-element.1707) | copy-start | bytes 3145732
  140.4 1.4 copy-start.8
  141.8 49.4 %all-gather.12.cloned.1.call-start = ((), (), s32[]{:S(2)}) async-start(), calls=%async_computation.8 | async-start | bytes 1310720 | tf_op jit(solution)/shard_map/all_gather | solution.py:113
  142.7 67.3 %all-gather.14.cloned.1.call-start = ((), (), s32[]{:S(2)}) async-start(), calls=%async_computation.9 | async-start | bytes 1310720 | tf_op jit(solution)/shard_map/all_gather | solution.py:114
  174.1 140.9 %reduce-scatter.11.cloned.1.call-start = ((), (), s32[]{:S(2)}) async-start(), calls=%async_computation.12 | async-start | bytes 2621440 | tf_op jit(solution)/shard_map/reduce_scatter | solution.py:179
  213.5 3.2 copy-start
  223.7 1.6 copy-start.2
  225.8 1.3 copy-start.3
  236.5 1.6 copy-start.2
  238.7 1.3 copy-start.3
  249.4 1.6 copy-start.2
  251.5 1.3 copy-start.3
  262.2 1.6 copy-start.2
  264.4 1.3 copy-start.3
  271.0 1.6 copy-start.4
  271.0 77.3 %reduce-scatter.7.cloned.1.call-start = ((), (), s32[]{:S(2)}) async-start(), calls=%async_computation.10 | async-start | bytes 2621440 | tf_op jit(solution)/shard_map/reduce_scatter | solution.py:174
  274.4 1.6 copy-start.6
  274.4 120.2 %reduce-scatter.9.cloned.1.call-start = ((), (), s32[]{:S(2)}) async-start(), calls=%async_computation.11 | async-start | bytes 2621440 | tf_op jit(solution)/shard_map/reduce_scatter | solution.py:178
  (2 other events, 2.3 us)
Sparse Core Ops, SparseCore 0:
  10.2 19.4 all-gather.7
  31.7 27.9 all-gather.5
  61.9 27.4 all-gather.9
  141.9 30.3 reduce-scatter.4
  174.4 16.7 all-gather.11
  193.2 16.7 all-gather.13
  271.1 43.8 reduce-scatter.10
  317.6 30.7 reduce-scatter.6
  350.7 43.8 reduce-scatter.8
where the time goes:
time: 405 us; the launch traced here: 403 us
  waiting for transfers between devices  223 us (55%)
  local copies, waits for them, and re-layouts  54.1 us (13%)
  other arithmetic  41 us (10%)
  matrix products  40.2 us (10%)
  blocking collectives  21.5 us (5%)
  between operations  14 us (3%)
  loops' own time  8.27 us (2%)
    reduce_scatter x1, waiting for transfers between devices, on_device(): lax.psum_scatter(key_parts, 'row', scatter_dimension=1, tiled=True)  44.5 us
    reduce_scatter x1, waiting for transfers between devices, on_device(): lax.psum_scatter(value_parts, 'row', scatter_dimension=1, tiled=True)  35.4 us
    reduce_scatter x1, waiting for transfers between devices, on_device(): lax.psum_scatter(query_parts, 'col', scatter_dimension=1, tiled=True)  31.5 us
    all_gather x1, waiting for transfers between devices, on_device(): lax.all_gather(keys, 'row', axis=1, tiled=True)  30.1 us
    reduce_scatter x1, waiting for transfers between devices, on_device(): lax.psum_scatter(partial_out, 'col', scatter_dimension=1, tiled=True)  29.6 us
    all_gather x1, waiting for transfers between devices, on_device(): lax.all_gather(out_share, 'col', axis=1, tiled=True)  18.8 us
    all_gather x1, waiting for transfers between devices, on_device(): lax.all_gather(cotangent, 'col', axis=1, tiled=True)  17 us
    all_gather x1, waiting for transfers between devices, on_device(): q_full = lax.all_gather(queries, 'col', axis=1, tiled=True)  16.3 us
  transfers between devices with their start and end apart: 9, of which 8 were waited for; matrix products, arithmetic and copies ran while one was open for 8% of the time, Pallas kernels for 0%

commit v1 on v0

--- a/solution.py
+++ b/solution.py
@@ -10,6 +10,18 @@
 BLK = 128
 MAXNB = 16
 NEG_FILL = -1e30
+
+
+def gather_by_bits(x, axis, dim):
+    ways, here, turn = (lax.axis_size(axis), lax.axis_index(axis), x.shape[dim])
+    line, have = (x, 1)
+    while have < ways:
+        line = jnp.concatenate(
+            [line, lax.ppermute(line, axis, [(d, (d - have) % ways) for d in range(ways)])],
+            axis=dim,
+        )
+        have = 2 * have
+    return jnp.roll(line, here * turn, axis=dim)
 
 
 def tile_scores(query_tile, key_tile, score_scale):
@@ -111,7 +123,7 @@
     )
     grad_full, out_full = (
         lax.all_gather(cotangent, "col", axis=1, tiled=True),
-        lax.all_gather(out_share, "col", axis=1, tiled=True),
+        gather_by_bits(out_share, "col", 1),
     )
     delta = jnp.einsum(
         "qhd,qhd->hq",

time: 405 us -> 398 us (0.983)
  waiting for transfers between devices: 223 us -> 211 us
    ppermute x0 -> x2, waiting for transfers between devices: none -> 21.4 us  [gather_by_bits(): lax.ppermute(line, axis, [(d, (d - have) % ways) for d in range(ways)])]
    all_gather x1 -> x0, waiting for transfers between devices: 18.8 us -> none  [on_device(): lax.all_gather(out_share, 'col', axis=1, tiled=True)]
    all_gather x1, waiting for transfers between devices: 17 us -> 0.01 us  [on_device(): lax.all_gather(cotangent, 'col', axis=1, tiled=True)]
    unnamed x23 -> x25, local copies, waits for them, and re-layouts: 12.4 us -> 14.4 us
  transfers between devices with their start and end apart: 9 -> 10, of which waited for: 8 -> 8; matrix products, arithmetic and copies ran while one was open for 8% -> 10% of each run, Pallas kernels for 0% -> 0%
where the time goes in v1:
time: 398 us; the launch traced here: 396 us
  waiting for transfers between devices  211 us (53%)
  local copies, waits for them, and re-layouts  57.1 us (14%)
  other arithmetic  41.1 us (10%)
  matrix products  40.3 us (10%)
  blocking collectives  21.5 us (5%)
  between operations  14.3 us (4%)
  loops' own time  8.56 us (2%)
    reduce_scatter x1, waiting for transfers between devices, on_device(): lax.psum_scatter(key_parts, 'row', scatter_dimension=1, tiled=True)  44.6 us
    reduce_scatter x1, waiting for transfers between devices, on_device(): lax.psum_scatter(value_parts, 'row', scatter_dimension=1, tiled=True)  37.9 us
    reduce_scatter x1, waiting for transfers between devices, on_device(): lax.psum_scatter(query_parts, 'col', scatter_dimension=1, tiled=True)  31.5 us
    all_gather x1, waiting for transfers between devices, on_device(): lax.all_gather(keys, 'row', axis=1, tiled=True)  30.1 us
    reduce_scatter x1, waiting for transfers between devices, on_device(): lax.psum_scatter(partial_out, 'col', scatter_dimension=1, tiled=True)  29.6 us
    ppermute x2, waiting for transfers between devices, gather_by_bits(): lax.ppermute(line, axis, [(d, (d - have) % ways) for d in range(ways)])  21.4 us
    all_gather x1, waiting for transfers between devices, on_device(): q_full = lax.all_gather(queries, 'col', axis=1, tiled=True)  16.3 us
    dot_general x4, matrix products, output_work(): jnp.einsum('hqk,khd->qhd', weights, value_heads, preferred_element_type=j...  15.3 us
  transfers between devices with their start and end apart: 10, of which 8 were waited for; matrix products, arithmetic and copies ran while one was open for 10% of the time, Pallas kernels for 0%

profile of v1, /device:TPU:0, one launch (start us, length us, event | category | flops | bytes accessed | tf_op | source)
XLA Modules:
  0.0 396.1 jit_solution(2193601332222021265)
XLA Ops:
  13.3 16.3 %all-gather.7.cloned.1.call-done = bf16[512,1024]{0,1:T(8,128)(2,1)} async-done(((bf16[512,256]{0,1:T(8,128)(2,1)}), bf16[512,1024]{0,1:T(8,128)(2,1)}) %all-gather.7.cloned.1.call-update) | async-done | bytes 1048592 | tf_op jit(solution)/shard_map/all_gather | solution.py:38
  29.6 30.1 %all-gather.5.cloned.1.call-done = bf16[512,1024]{0,1:T(8,128)(2,1)} async-done(((bf16[512,256]{0,1:T(8,128)(2,1)}), bf16[512,1024]{0,1:T(8,128)(2,1)}) %all-gather.5.cloned.1.call-update) | async-done | bytes 1048592 | tf_op jit(solution)/shard_map/all_gather | solution.py:40
  59.7 22.0 %while.57 = (s32[]{:T(128)}, f32[16,512]{1,0:T(8,128)S(1)}, f32[16,512]{1,0:T(8,128)S(1)}, pred[1,4]{1,0:T(4,128)(4,1)S(1)}, bf16[512,1024]{0,1:T(8,128)(2,1)}, ...) while((s32[]{:T(128)}, f32[16,512]{1,0:T(8,128)S(1)}, ...), condition=%wide.region_7.8_spmd.clone, body=%wide.region_2.7_spmd.clone.sunk | while | flops 142622736 | bytes 10658168 | solution.py:93
  60.4 4.8 %conditional.9 = ((f32[16,512]{1,0:T(8,128)S(1)}, f32[16,512]{1,0:T(8,128)S(1)})) conditional(s32[]{:T(128)} %bitcast.68, (f32[16,512]{1,0:T(8,128)S(1)}, f32[16,512]{1,0:T(8,128)S(1)}) %tuple.195, (pred[4,4]{1,0:T(4,128)(4,1)S(1)}, s32[]{:T(128)}, s32[]{:T(128)}, bf16[512,1024]{0,1:T(8,128)(2,1)}, bf16[512,1024]{0,1:T(8,128)(2,1)}, ...), branch_computations={%region_3.3_spmd, %region_4.6_spmd} | conditional | flops 142622720 | bytes 10657886 | solution.py:89
  65.9 4.9 %conditional.9 = ((f32[16,512]{1,0:T(8,128)S(1)}, f32[16,512]{1,0:T(8,128)S(1)})) conditional(s32[]{:T(128)} %bitcast.68, (f32[16,512]{1,0:T(8,128)S(1)}, f32[16,512]{1,0:T(8,128)S(1)}) %tuple.195, (pred[4,4]{1,0:T(4,128)(4,1)S(1)}, s32[]{:T(128)}, s32[]{:T(128)}, bf16[512,1024]{0,1:T(8,128)(2,1)}, bf16[512,1024]{0,1:T(8,128)(2,1)}, ...), branch_computations={%region_3.3_spmd, %region_4.6_spmd} | conditional | flops 142622720 | bytes 10657886 | solution.py:89
  71.4 4.8 %conditional.9 = ((f32[16,512]{1,0:T(8,128)S(1)}, f32[16,512]{1,0:T(8,128)S(1)})) conditional(s32[]{:T(128)} %bitcast.68, (f32[16,512]{1,0:T(8,128)S(1)}, f32[16,512]{1,0:T(8,128)S(1)}) %tuple.195, (pred[4,4]{1,0:T(4,128)(4,1)S(1)}, s32[]{:T(128)}, s32[]{:T(128)}, bf16[512,1024]{0,1:T(8,128)(2,1)}, bf16[512,1024]{0,1:T(8,128)(2,1)}, ...), branch_computations={%region_3.3_spmd, %region_4.6_spmd} | conditional | flops 142622720 | bytes 10657886 | solution.py:89
  76.9 4.8 %conditional.9 = ((f32[16,512]{1,0:T(8,128)S(1)}, f32[16,512]{1,0:T(8,128)S(1)})) conditional(s32[]{:T(128)} %bitcast.68, (f32[16,512]{1,0:T(8,128)S(1)}, f32[16,512]{1,0:T(8,128)S(1)}) %tuple.195, (pred[4,4]{1,0:T(4,128)(4,1)S(1)}, s32[]{:T(128)}, s32[]{:T(128)}, bf16[512,1024]{0,1:T(8,128)(2,1)}, bf16[512,1024]{0,1:T(8,128)(2,1)}, ...), branch_computations={%region_3.3_spmd, %region_4.6_spmd} | conditional | flops 142622720 | bytes 10657886 | solution.py:89
  81.8 11.3 %pmax.7 = bf16[16,512]{1,0:T(8,128)(2,1)S(1)} all-reduce(bf16[16,512]{1,0:T(8,128)(2,1)S(1)} %convert_element_type.89), channel_id=1, replica_groups=mesh['groups'=2,'row'=4,'col'=4] {'col'}, use_global_device_ids=true, to_apply=%region_8.9 | all-reduce | flops 8192 | bytes 32768 | tf_op jit(solution)/shard_map/pmax | solution.py:94
  93.1 10.3 %psum.7 = f32[16,512]{1,0:T(8,128)S(1)} all-reduce(f32[16,512]{1,0:T(8,128)S(1)} %exponential_multiply_fusion), channel_id=1, replica_groups=mesh['groups'=2,'row'=4,'col'=4] {'col'}, use_global_device_ids=true, to_apply=%region_9.10 | all-reduce | flops 8192 | bytes 65536 | tf_op jit(solution)/shard_map/psum | solution.py:95
  103.6 36.9 %while.58 = (s32[]{:T(128)}, f32[512,1024]{0,1:T(8,128)S(1)}, pred[1,4]{1,0:T(4,128)(4,1)S(1)}, bf16[512,1024]{0,1:T(8,128)(2,1)}, bf16[512,1024]{0,1:T(8,128)(2...) while((s32[]{:T(128)}, f32[512,1024]{0,1:T(8,128)S(1)}, ...), condition=%wide.region_13.14_spmd.clone, body=%wide.region_10.13_spmd.clone.sunk | while | flops 275251200 | bytes 11083640 | solution.py:120
  104.3 8.6 %conditional.10 = (f32[512,1024]{0,1:T(8,128)S(1)}) conditional(s32[]{:T(128)} %bitcast.69, f32[512,1024]{0,1:T(8,128)S(1)} %get-tuple-element.1619, (pred[4,4]{1,0:T(4,128)(4,1)S(1)}, s32[]{:T(128)}, s32[]{:T(128)}, bf16[512,1024]{0,1:T(8,128)(2,1)}, bf16[512,1024]{0,1:T(8,128)(2,1)S(1)}, /*index=5*/f32[16,512]{1,0:T(8,128)S(1)}, ...), branch_computations={%region_11.11_spmd, %region_12.12_spmd} | conditional | flops 275251200 | bytes 11083342 | solution.py:118
  113.5 8.6 %conditional.10 = (f32[512,1024]{0,1:T(8,128)S(1)}) conditional(s32[]{:T(128)} %bitcast.69, f32[512,1024]{0,1:T(8,128)S(1)} %get-tuple-element.1619, (pred[4,4]{1,0:T(4,128)(4,1)S(1)}, s32[]{:T(128)}, s32[]{:T(128)}, bf16[512,1024]{0,1:T(8,128)(2,1)}, bf16[512,1024]{0,1:T(8,128)(2,1)S(1)}, /*index=5*/f32[16,512]{1,0:T(8,128)S(1)}, ...), branch_computations={%region_11.11_spmd, %region_12.12_spmd} | conditional | flops 275251200 | bytes 11083342 | solution.py:118
  122.8 8.6 %conditional.10 = (f32[512,1024]{0,1:T(8,128)S(1)}) conditional(s32[]{:T(128)} %bitcast.69, f32[512,1024]{0,1:T(8,128)S(1)} %get-tuple-element.1619, (pred[4,4]{1,0:T(4,128)(4,1)S(1)}, s32[]{:T(128)}, s32[]{:T(128)}, bf16[512,1024]{0,1:T(8,128)(2,1)}, bf16[512,1024]{0,1:T(8,128)(2,1)S(1)}, /*index=5*/f32[16,512]{1,0:T(8,128)S(1)}, ...), branch_computations={%region_11.11_spmd, %region_12.12_spmd} | conditional | flops 275251200 | bytes 11083342 | solution.py:118
  132.0 8.6 %conditional.10 = (f32[512,1024]{0,1:T(8,128)S(1)}) conditional(s32[]{:T(128)} %bitcast.69, f32[512,1024]{0,1:T(8,128)S(1)} %get-tuple-element.1619, (pred[4,4]{1,0:T(4,128)(4,1)S(1)}, s32[]{:T(128)}, s32[]{:T(128)}, bf16[512,1024]{0,1:T(8,128)(2,1)}, bf16[512,1024]{0,1:T(8,128)(2,1)S(1)}, /*index=5*/f32[16,512]{1,0:T(8,128)S(1)}, ...), branch_computations={%region_11.11_spmd, %region_12.12_spmd} | conditional | flops 275251200 | bytes 11083342 | solution.py:118
  142.9 29.6 %reduce-scatter.5.cloned.1.call-done = f32[512,256]{0,1:T(8,128)} async-done(((f32[512,1024]{0,1:T(8,128)}), f32[512,256]{0,1:T(8,128)}) %reduce-scatter.5.cloned.1.call-update) | async-done | bytes 524304 | tf_op jit(solution)/shard_map/reduce_scatter | solution.py:121
  180.4 17.5 %collective-permute-done.1 = bf16[512,512]{0,1:T(8,128)(2,1)S(1)} collective-permute-done((bf16[512,512]{0,1:T(8,128)(2,1)S(1)}, bf16[512,512]{0,1:T(8,128)(2,1)S(1)}, u32[]{:S(2)}, u32[]{:S(2)}) %collective-permute-start.1) | collective-permute-done | bytes 524320 | tf_op jit(solution)/shard_map/ppermute | solution.py:20
  207.7 51.7 %while.59 = (s32[]{:T(128)}, f32[512,1024]{0,1:T(8,128)}, f32[512,1024]{0,1:T(8,128)}, f32[512,1024]{0,1:T(8,128)}, pred[1,4]{1,0:T(4,128)(4,1)S(1)}, /*index=5*...) while((s32[]{:T(128)}, f32[512,1024]{0,1:T(8,128)}, ...), condition=%wide.region_18.19_spmd.clone, body=%wide.region_15.18_spmd.clone.sunk | while | flops 683016192 | bytes 48078884 | solution.py:185
  208.2 12.3 %conditional.11 = ((f32[512,1024]{0,1:T(8,128)}, f32[512,1024]{0,1:T(8,128)}, f32[512,1024]{0,1:T(8,128)})) conditional(s32[]{:T(128)} %bitcast.70, (f32[512,1024]{0,1:T(8,128)}, f32[512,1024]{0,1:T(8,128)}, f32[512,1024]{0,1:T(8,128)}) %tuple.200, (pred[4,4]{1,0:T(4,128)(4,1)S(1)}, s32[]{:T(128)}, s32[]{:T(128)}, bf16[512,1024]{0,1:T(8,128)(2,1)}, ...), branch_computations={%region_16.16_spmd, %region_17.17_spmd} | conditional | flops 683016192 | bytes 48078500 | solution.py:178
  221.2 12.4 %conditional.11 = ((f32[512,1024]{0,1:T(8,128)}, f32[512,1024]{0,1:T(8,128)}, f32[512,1024]{0,1:T(8,128)})) conditional(s32[]{:T(128)} %bitcast.70, (f32[512,1024]{0,1:T(8,128)}, f32[512,1024]{0,1:T(8,128)}, f32[512,1024]{0,1:T(8,128)}) %tuple.200, (pred[4,4]{1,0:T(4,128)(4,1)S(1)}, s32[]{:T(128)}, s32[]{:T(128)}, bf16[512,1024]{0,1:T(8,128)(2,1)}, ...), branch_computations={%region_16.16_spmd, %region_17.17_spmd} | conditional | flops 683016192 | bytes 48078500 | solution.py:178
  234.1 12.3 %conditional.11 = ((f32[512,1024]{0,1:T(8,128)}, f32[512,1024]{0,1:T(8,128)}, f32[512,1024]{0,1:T(8,128)})) conditional(s32[]{:T(128)} %bitcast.70, (f32[512,1024]{0,1:T(8,128)}, f32[512,1024]{0,1:T(8,128)}, f32[512,1024]{0,1:T(8,128)}) %tuple.200, (pred[4,4]{1,0:T(4,128)(4,1)S(1)}, s32[]{:T(128)}, s32[]{:T(128)}, bf16[512,1024]{0,1:T(8,128)(2,1)}, ...), branch_computations={%region_16.16_spmd, %region_17.17_spmd} | conditional | flops 683016192 | bytes 48078500 | solution.py:178
  247.0 12.4 %conditional.11 = ((f32[512,1024]{0,1:T(8,128)}, f32[512,1024]{0,1:T(8,128)}, f32[512,1024]{0,1:T(8,128)})) conditional(s32[]{:T(128)} %bitcast.70, (f32[512,1024]{0,1:T(8,128)}, f32[512,1024]{0,1:T(8,128)}, f32[512,1024]{0,1:T(8,128)}) %tuple.200, (pred[4,4]{1,0:T(4,128)(4,1)S(1)}, s32[]{:T(128)}, s32[]{:T(128)}, bf16[512,1024]{0,1:T(8,128)(2,1)}, ...), branch_computations={%region_16.16_spmd, %region_17.17_spmd} | conditional | flops 683016192 | bytes 48078500 | solution.py:178
  270.0 37.9 %reduce-scatter.11.cloned.1.call-done = f32[512,256]{1,0:T(8,128)} async-done(((f32[512,1024]{1,0:T(8,128)}), f32[512,256]{1,0:T(8,128)}) %reduce-scatter.11.cloned.1.call-update) | async-done | bytes 524304 | tf_op jit(solution)/shard_map/reduce_scatter | solution.py:191
  309.7 31.5 %reduce-scatter.7.cloned.1.call-done = f32[512,256]{1,0:T(8,128)} async-done(((f32[512,1024]{1,0:T(8,128)}), f32[512,256]{1,0:T(8,128)}) %reduce-scatter.7.cloned.1.call-update) | async-done | bytes 524304 | tf_op jit(solution)/shard_map/reduce_scatter | solution.py:186
  343.0 44.6 %reduce-scatter.9.cloned.1.call-done = f32[512,256]{1,0:T(8,128)} async-done(((f32[512,1024]{1,0:T(8,128)}), f32[512,256]{1,0:T(8,128)}) %reduce-scatter.9.cloned.1.call-update) | async-done | bytes 524304 | tf_op jit(solution)/shard_map/reduce_scatter | solution.py:190
  (205 shorter events, 144.4 us)
Async XLA Ops:
  7.2 5.7 %copy-start.9 = (s32[4]{0:T(128)S(1)}, s32[4]{0:T(128)}, u32[]{:S(2)}) copy-start(s32[4]{0:T(128)} %param.23) | copy-start | bytes 52
  7.2 5.8 %copy-start.8 = (s32[4,16]{1,0:T(4,128)S(1)}, s32[4,16]{1,0:T(4,128)}, u32[]{:S(2)}) copy-start(s32[4,16]{1,0:T(4,128)} %param.22) | copy-start | bytes 772
  7.2 22.4 %all-gather.7.cloned.1.call-start = ((), (), s32[]{:S(2)}) async-start(), calls=%async_computation.5 | async-start | bytes 1310720 | tf_op jit(solution)/shard_map/all_gather | solution.py:38
  9.1 50.7 %all-gather.5.cloned.1.call-start = ((), (), s32[]{:S(2)}) async-start(), calls=%async_computation.4 | async-start | bytes 1310720 | tf_op jit(solution)/shard_map/all_gather | solution.py:40
  10.9 92.4 %all-gather.9.cloned.1.call-start = ((), (), s32[]{:S(2)}) async-start(), calls=%async_computation.6 | async-start | bytes 1310720 | tf_op jit(solution)/shard_map/all_gather | solution.py:41
  12.8 159.7 %reduce-scatter.5.cloned.1.call-start = ((), (), s32[]{:S(2)}) async-start(), calls=%async_computation.7 | async-start | bytes 2621440 | tf_op jit(solution)/shard_map/reduce_scatter | solution.py:121
  81.8 21.9 %copy-start.1 = (bf16[512,1024]{0,1:T(8,128)(2,1)S(1)}, bf16[512,1024]{0,1:T(8,128)(2,1)}, u32[]{:S(2)}) copy-start(bf16[512,1024]{0,1:T(8,128)(2,1)} %get-tuple-element.1708) | copy-start | bytes 3145732
  140.6 1.4 copy-start.7
  141.9 59.1 %all-gather.11.cloned.1.call-start = ((), (), s32[]{:S(2)}) async-start(), calls=%async_computation.8 | async-start | bytes 1310720 | tf_op jit(solution)/shard_map/all_gather | solution.py:125
  142.8 165.1 %reduce-scatter.11.cloned.1.call-start = ((), (), s32[]{:S(2)}) async-start(), calls=%async_computation.11 | async-start | bytes 2621440 | tf_op jit(solution)/shard_map/reduce_scatter | solution.py:191
  174.2 3.9 collective-permute-start
  178.2 19.7 %collective-permute-start.1 = (bf16[512,512]{0,1:T(8,128)(2,1)S(1)}, bf16[512,512]{0,1:T(8,128)(2,1)S(1)}, u32[]{:S(2)}, u32[]{:S(2)}) collective-permute-start(bf16[512,512]{0,1:T(8,128)(2,1)S(1)} %pad_maximum_fusion), channel_id=1, source_target_pairs={{0,2},{1,3},{2,0},{3,1},{4,6},{5,7},{6,4},{7,5},{8,10},{9,11},{10,... | collective-permute-start | bytes 1572872 | tf_op jit(solution)/shard_map/ppermute | solution.py:20
  204.5 3.2 copy-start
  214.8 1.6 copy-start.2
  216.9 1.3 copy-start.3
  227.7 1.6 copy-start.2
  229.8 1.3 copy-start.3
  240.7 1.6 copy-start.2
  242.8 1.3 copy-start.3
  253.6 1.6 copy-start.2
  262.3 1.6 copy-start.4
  262.4 78.8 %reduce-scatter.7.cloned.1.call-start = ((), (), s32[]{:S(2)}) async-start(), calls=%async_computation.9 | async-start | bytes 2621440 | tf_op jit(solution)/shard_map/reduce_scatter | solution.py:186
  265.8 1.6 copy-start.6
  265.8 121.7 %reduce-scatter.9.cloned.1.call-start = ((), (), s32[]{:S(2)}) async-start(), calls=%async_computation.10 | async-start | bytes 2621440 | tf_op jit(solution)/shard_map/reduce_scatter | solution.py:190
  (2 other events, 2.7 us)
Sparse Core Ops, SparseCore 0:
  10.2 19.4 all-gather.6
  31.7 27.9 all-gather.4
  61.9 27.4 all-gather.8
  142.0 30.3 reduce-scatter.4
  174.5 22.4 all-gather.10
  262.5 45.3 reduce-scatter.10
  310.4 30.7 reduce-scatter.6
  343.6 43.8 reduce-scatter.8
